TPU v7x, 32 devices: a whole 2x2x4 slice. The times are simulated.
32 devices in a mesh: dp: 16 (over z, y, x), tensor: 2 (over core).
Axes of the slice: x: 2, y: 2, z: 4, core: 2. Of those that a mesh axis runs over, the one named last changes fastest.
Arguments:
- tokens: bfloat16 [4096, 1024], P(('dp', 'tensor')), may hold values from -6 to 6
- cotangent: bfloat16 [4096, 1024], P(('dp', 'tensor')), may hold values from -6 to 6
- lengths: int32 [16], P('dp'), may hold values from 64 to 256, as said below
- w_query: bfloat16 [1024, 2048], P('dp', 'tensor'), may hold values from -0.1875 to 0.1875
- key_matrix: bfloat16 [1024, 1024], P('dp', 'tensor'), may hold values from -0.1875 to 0.1875
- value_matrix: bfloat16 [1024, 1024], P('dp', 'tensor'), may hold values from -0.1875 to 0.1875
- w_out: bfloat16 [1024, 2048], P('dp', 'tensor'), may hold values from -0.375 to 0.375
- w_gate: bfloat16 [1024, 3072], P('dp', 'tensor'), may hold values from -0.1875 to 0.1875
- w_up: bfloat16 [1024, 3072], P('dp', 'tensor'), may hold values from -0.1875 to 0.1875
- w_down: bfloat16 [1024, 3072], P('dp', 'tensor'), may hold values from -0.109375 to 0.109375
- gain_attn: float32 [1024], replicated, may hold values from 0.5 to 2
- gain_mlp: float32 [1024], replicated, may hold values from 0.5 to 2
- gain_query: float32 [128], replicated, may hold values from 0.5 to 2
- gain_key: float32 [128], replicated, may hold values from 0.5 to 2
Outputs:
- result: bfloat16 [4096, 1024], P(('dp', 'tensor'))
- grad_tokens: float32 [4096, 1024], P(('dp', 'tensor'))
- grad_w_query: float32 [1024, 2048], P('dp', 'tensor')
- grad_w_key: float32 [1024, 1024], P('dp', 'tensor')
- grad_w_value: float32 [1024, 1024], P('dp', 'tensor')
- grad_w_out: float32 [1024, 2048], P('dp', 'tensor')
- grad_w_gate: float32 [1024, 3072], P('dp', 'tensor')
- grad_w_up: float32 [1024, 3072], P('dp', 'tensor')
- grad_w_down: float32 [1024, 3072], P('dp', 'tensor')
- grad_gain_attn: float32 [1024], replicated
- grad_gain_mlp: float32 [1024], replicated
- grad_gain_query: float32 [128], replicated
- grad_gain_key: float32 [128], replicated
Inputs may be any that keep to these rules, and one draw needn't show every extreme that they name: `lengths`: some sequence fills all 256 token slots of its block.
All inputs are finite; a program needn't handle non-finite values.
Results may differ from a plain program's by a relative error of at most 0.013.
The roundings to bfloat16 on the way count: a program that leaves them out, or rounds other values in their place, can miss the bound.
Values may be sent and summed in bfloat16 or wider, within the bound.
A program may use at most 128 MiB of HBM per device.

v0:
```python
import functools
import math

import jax
import jax.numpy as jnp
from jax import lax
from jax.experimental import pallas as pl
from jax.experimental.pallas import tpu as pltpu
from jax.sharding import PartitionSpec as P

MESH = pl.DeviceIdType.MESH
VMEM_LIMIT = 64000000

HEAD_SIZE = 128


norm_eps = 1e-06
rope_base = 1000000.0


def rms_rows(values, gain_vec):
    inverse = lax.rsqrt(jnp.mean(values * values, axis=-1, keepdims=True) + norm_eps)
    return (values * inverse * gain_vec, inverse)


def rms_back(grad_output, values, inverse, gain_vec):
    scaled = grad_output * gain_vec
    mean_term = jnp.mean(scaled * values, axis=-1, keepdims=True)
    grad_values = inverse * scaled - values * (inverse * inverse * inverse) * mean_term
    flat_terms = (grad_output * values * inverse).reshape(-1, values.shape[-1])
    return (grad_values, jnp.sum(flat_terms, axis=0))


def rope_tables(positions, head_width):
    half_width = head_width // 2
    frequency = jnp.exp(
        -jnp.log(rope_base) * (2.0 * jnp.arange(half_width, dtype=jnp.float32) / head_width)
    )
    angles = positions.astype(jnp.float32)[:, None] * frequency[None, :]
    return (jnp.cos(angles), jnp.sin(angles))


def product_t(left, right):
    return lax.dot_general(
        left, right, (((1,), (1,)), ((), ())), preferred_element_type=jnp.float32
    )


def product_tn(left, right):
    return lax.dot_general(
        left, right, (((0,), (0,)), ((), ())), preferred_element_type=jnp.float32
    )


def split_dims(count):
    return (count // 8, 2, 2, 2)


PAIR = 1
AHEAD = 5
DEPTH = 2
RUN = 3
LAG = 2
INNER = ((0, 2, 3), (0, 3, 2))


def pieces(layouts):
    chunks = []
    for out_index, members in enumerate(layouts):
        column = 0
        for index, half in members:
            step = math.gcd(half, 256)
            parts = half // step
            for part in range(parts):
                order = INNER[len(chunks) % len(INNER)]
                chunks.append((index, part * step, step, out_index, column + part * step, order))
            column += half
    return chunks


class Place:
    def __init__(self, sizes):
        self.sizes = sizes
        self.me = lax.axis_index("dp")
        self.strides = [math.prod(sizes[i + 1 :]) for i in range(len(sizes))]
        self.coords = [
            lax.rem(lax.div(self.me, stride), size) for stride, size in zip(self.strides, sizes)
        ]
        self.base = [sum(size - 1 for size in sizes[:i]) for i in range(len(sizes))]

    def other(self, dim, offset):
        return lax.rem(self.coords[dim] + offset, self.sizes[dim])

    def peer(self, dim, offset):
        return self.me + (self.other(dim, offset) - self.coords[dim]) * self.strides[dim]

    def slot(self, dim, offset):
        return self.base[dim] + offset - 1

    def barrier(self, extra=()):
        barrier = pltpu.get_barrier_semaphore()
        count = 0
        for dim, size in enumerate(self.sizes):
            for offset in range(1, size):
                pl.semaphore_signal(
                    barrier, inc=1, device_id={"dp": self.peer(dim, offset)}, device_id_type=MESH
                )
                count += 1
        for target in extra:
            pl.semaphore_signal(barrier, inc=1, device_id=target, device_id_type=MESH)
            count += 1
        pl.semaphore_wait(barrier, count)


def remote(source, target, send, recv, device):
    return pltpu.make_async_remote_copy(
        src_ref=source,
        dst_ref=target,
        send_sem=send,
        recv_sem=recv,
        device_id=device,
        device_id_type=MESH,
    )


def gather_kernel(sizes, chunks, counts, *refs):
    n_in, n_out, n_rows = counts
    refs = list(refs)
    ins = [refs.pop(0) for _ in range(n_in)]
    row_ins = [refs.pop(0) for _ in range(n_rows)]
    length_in = refs.pop(0)
    outs = [refs.pop(0) for _ in range(n_out)]
    row_outs = [refs.pop(0) for _ in range(n_rows)]
    length_out = refs.pop(0)
    send_sem, recv_sem, local_sem, row_send, row_recv, length_sem = refs
    place = Place(sizes)
    k = len(sizes)
    mine = place.coords[PAIR]
    theirs = place.other(PAIR, 1)
    tensor_me = lax.axis_index("tensor")
    near = {"tensor": 1 - tensor_me}
    far = {"dp": place.peer(PAIR, 1)}

    def region(chunk, done, dim=None, coord=None):
        where = []
        for i in range(k):
            if i == dim:
                where.append(coord)
            elif i in done:
                where.append(slice(None))
            else:
                where.append(place.coords[i])
        return outs[chunk[3]].at[tuple(where) + (slice(None), pl.ds(chunk[4], chunk[2]))]

    def source_of(chunk, half_index):
        half = ins[chunk[0]].shape[1] // 2
        start = pl.multiple_of(half_index * half + chunk[1], 128)
        return ins[chunk[0]].at[:, pl.ds(start, chunk[2])]

    def steps(chunk):
        return (PAIR,) + chunk[5]

    def sends(j, stage):
        chunk = chunks[j]
        order = steps(chunk)
        dim, done = order[stage], order[:stage]
        block = region(chunk, done)
        source = source_of(chunk, theirs) if stage == 0 else block
        return [
            remote(
                source,
                block,
                send_sem.at[j, place.slot(dim, offset)],
                recv_sem.at[j, place.slot(dim, offset)],
                {"dp": place.peer(dim, offset)},
            )
            for offset in range(1, sizes[dim])
        ]

    def wait_arrivals(j, stage):
        chunk = chunks[j]
        order = steps(chunk)
        dim, done = order[stage], order[:stage]
        for offset in range(1, sizes[dim]):
            block = region(chunk, done, dim, place.other(dim, sizes[dim] - offset))
            remote(
                block,
                block,
                send_sem.at[j, place.slot(dim, offset)],
                recv_sem.at[j, place.slot(dim, offset)],
                {"dp": place.peer(dim, offset)},
            ).wait_recv()

    place.barrier([near])
    started, own = [], []
    crossing = remote(
        length_in, length_out.at[mine], length_sem.at[0], length_sem.at[1], far
    )
    crossing.start()
    rows_far, rows_near, passed = [], [], []

    def send_rows(i):
        slot = row_outs[i].at[mine, tensor_me]
        rows_far.append(remote(row_ins[i], slot, row_send.at[i, 0], row_recv.at[i, 0], far))
        rows_near.append(remote(row_ins[i], slot, row_send.at[i, 1], row_recv.at[i, 1], near))
        rows_far[-1].start()
        rows_near[-1].start()
        row_outs[i][mine, tensor_me] = row_ins[i][...]

    def pass_rows(i):
        rows_far[i].wait()
        slot = row_outs[i].at[theirs, tensor_me]
        passed.append(remote(slot, slot, row_send.at[i, 2], row_recv.at[i, 2], near))
        passed[-1].start()

    def begin(j):
        copies = sends(j, 0)
        for copy in copies:
            copy.start()
        started.extend(copies)
        copy = pltpu.make_async_copy(
            source_of(chunks[j], mine), region(chunks[j], ()), local_sem.at[j]
        )
        copy.start()
        own.append(copy)

    for j in range(min(AHEAD, len(chunks))):
        begin(j)
    length_out[mine] = length_in[...]
    total_steps = len(chunks) + DEPTH * (k - 1)
    for step in range(total_steps):
        if step + AHEAD < len(chunks):
            begin(step + AHEAD)
        for i in range(n_rows):
            if step == min(4 + 3 * i, total_steps - 1):
                send_rows(i)
        for stage in range(k, 0, -1):
            j = step - DEPTH * (stage - 1)
            if not 0 <= j < len(chunks):
                continue
            if stage == 1:
                own[j].wait()
            wait_arrivals(j, stage - 1)
            if stage < k:
                copies = sends(j, stage)
                for copy in copies:
                    copy.start()
                started += copies
        for i in range(n_rows):
            if step == min(12 + i, total_steps - 1):
                pass_rows(i)
    crossing.wait()
    for copy in rows_near + passed:
        copy.wait()
    for copy in started:
        copy.wait_send()


def gather_all(weights, layouts, rows, length_row, collective_id):
    sizes = split_dims(lax.axis_size("dp"))
    chunks = pieces(layouts)
    peers = sum(size - 1 for size in sizes)
    n_in, n_out, n_rows = len(weights), len(layouts), len(rows)
    depth = weights[0].shape[0]
    whole = pl.BlockSpec(memory_space=pltpu.VMEM)
    outs = pl.pallas_call(
        functools.partial(gather_kernel, sizes, chunks, (n_in, n_out, n_rows)),
        out_shape=[
            jax.ShapeDtypeStruct(sizes + (depth, sum(half for _, half in members)), jnp.bfloat16)
            for members in layouts
        ]
        + [jax.ShapeDtypeStruct((2, 2) + r.shape, r.dtype) for r in rows]
        + [jax.ShapeDtypeStruct((2,) + length_row.shape, length_row.dtype)],
        in_specs=[whole] * (n_in + n_rows + 1),
        out_specs=[pl.BlockSpec(memory_space=pl.ANY)] * n_out + [whole] * (n_rows + 1),
        scratch_shapes=[
            pltpu.SemaphoreType.DMA((len(chunks), peers)),
            pltpu.SemaphoreType.DMA((len(chunks), peers)),
            pltpu.SemaphoreType.DMA((len(chunks),)),
            pltpu.SemaphoreType.DMA((n_rows, 3)),
            pltpu.SemaphoreType.DMA((n_rows, 3)),
            pltpu.SemaphoreType.DMA((2,)),
        ],
        compiler_params=pltpu.CompilerParams(
            collective_id=collective_id, has_side_effects=True, vmem_limit_bytes=VMEM_LIMIT
        ),
    )(*weights, *rows, length_row)
    full = [out.reshape(-1, out.shape[-1]) for out in outs[:n_out]]
    row_sets = [out.reshape(-1, out.shape[-1]) for out in outs[n_out : n_out + n_rows]]
    return full, row_sets, outs[n_out + n_rows][:, 0, 0]


def reduce_kernel(sizes, chunks, counts, tensor_size, *refs):
    n_in, n_out = counts
    refs = list(refs)
    ins = [refs.pop(0) for _ in range(n_in)]
    gains = refs.pop(0)
    outs = [refs.pop(0) for _ in range(n_out)]
    gain_out = refs.pop(0)
    k = len(sizes)
    m = k - 1
    held = [[refs.pop(0) for _ in range(m - 1)] for _ in chunks]
    landed = [[refs.pop(0) for _ in range(m)] for _ in chunks]
    crossed = [refs.pop(0) for _ in chunks]
    gain_held = [refs.pop(0) for _ in range(k)]
    gain_landed = [refs.pop(0) for _ in range(k + 1)]
    send_sem, recv_sem, local_sem, gain_send, gain_recv = refs
    place = Place(sizes)
    tensor_me = lax.axis_index("tensor")
    mine = place.coords[PAIR]
    theirs = place.other(PAIR, 1)
    rows = ins[0].shape[-2]

    def order_of(j):
        return tuple(reversed(chunks[j][5]))

    def part(ref, dims, dim, coord, columns):
        where = tuple(coord if i == dim else slice(None) for i in dims)
        return ref.at[where + (slice(None), columns)]

    def copies_of(j, stage):
        _, _, width, array, column, _ = chunks[j]
        order = order_of(j)
        dim = order[stage]
        dims = [i for i in range(k) if i not in order[:stage]]
        if stage == 0:
            ref, columns = ins[array], pl.ds(column, width)
        else:
            ref, columns = held[j][stage - 1], slice(None)
        return [
            remote(
                part(ref, dims, dim, place.other(dim, offset), columns),
                landed[j][stage].at[offset - 1],
                send_sem.at[j, place.slot(dim, offset)],
                recv_sem.at[j, place.slot(dim, offset)],
                {"dp": place.peer(dim, offset)},
            )
            for offset in range(1, sizes[dim])
        ]

    def result_at(j):
        index, start, width = chunks[j][:3]
        half = outs[index].shape[1] // 2
        return outs[index], pl.ds(pl.multiple_of(mine * half + start, 128), width)

    def cross_copy(j):
        out, columns = result_at(j)
        slot = place.slot(PAIR, 1)
        return remote(
            crossed[j],
            out.at[:, columns],
            send_sem.at[j, slot],
            recv_sem.at[j, slot],
            {"dp": place.peer(PAIR, 1)},
        )

    def add_up(j, stage):
        order = order_of(j)
        dim = order[stage]
        dims = [i for i in range(k) if i not in order[:stage]]
        lead = [sizes[i] for i in dims if i != dim]
        per = rows // 16

        def total_of(where, rows_at):
            if stage == 0:
                own = tuple(where)
                source = held[j][0]
            else:
                own = list(where)
                own.insert(dims.index(dim), place.coords[dim])
                own = tuple(own)
                source = held[j][stage - 1]
            total = source[own + (rows_at, slice(None))].astype(jnp.float32)
            for offset in range(1, sizes[dim]):
                got = landed[j][stage][(offset - 1,) + tuple(where) + (rows_at, slice(None))]
                total = total + got.astype(jnp.float32)
            return total

        if stage == m - 1:

            def last(i, carry):
                rows_at = pl.ds(pl.multiple_of(i * 16, 16), 16)
                crossed[j][rows_at, :] = total_of((theirs,), rows_at)
                return carry

            lax.fori_loop(0, per, last, 0)
            copy = cross_copy(j)
            copy.start()

            def keep(i, carry):
                rows_at = pl.ds(pl.multiple_of(i * 16, 16), 16)
                out, columns = result_at(j)
                out[rows_at, columns] = total_of((mine,), rows_at)
                return carry

            lax.fori_loop(0, per, keep, 0)
            return copy

        def body(i, carry):
            rows_at = pl.ds(pl.multiple_of(lax.rem(i, per) * 16, 16), 16)
            flat = lax.div(i, per)
            where = []
            for position in range(len(lead)):
                below = math.prod(lead[position + 1 :])
                where.append(lax.rem(lax.div(flat, below), lead[position]))
            total = total_of(where, rows_at)
            held[j][stage][tuple(where) + (rows_at, slice(None))] = total.astype(jnp.bfloat16)
            return carry

        lax.fori_loop(0, math.prod(lead) * per, body, 0)
        return None

    def gain_copies(stage):
        source = gains if stage == 0 else gain_held[stage - 1]
        result = []
        if stage < k:
            for offset in range(1, sizes[stage]):
                slot = place.slot(stage, offset)
                result.append(
                    remote(
                        source,
                        gain_landed[stage].at[offset - 1],
                        gain_send.at[slot],
                        gain_recv.at[slot],
                        {"dp": place.peer(stage, offset)},
                    )
                )
        else:
            first = sum(size - 1 for size in sizes)
            for offset in range(1, tensor_size):
                result.append(
                    remote(
                        source,
                        gain_landed[stage].at[offset - 1],
                        gain_send.at[first + offset - 1],
                        gain_recv.at[first + offset - 1],
                        {"tensor": lax.rem(tensor_me + offset, tensor_size)},
                    )
                )
        return result

    place.barrier(
        [{"tensor": lax.rem(tensor_me + i, tensor_size)} for i in range(1, tensor_size)]
    )
    flights, own, crossing = [], [], []

    def begin(j):
        _, _, width, array, column, _ = chunks[j]
        first = copies_of(j, 0)
        for copy in first:
            copy.start()
        flights.append([first])
        dim = order_of(j)[0]
        copy = pltpu.make_async_copy(
            part(ins[array], range(k), dim, place.coords[dim], pl.ds(column, width)),
            held[j][0],
            local_sem.at[j],
        )
        copy.start()
        own.append(copy)

    for j in range(min(RUN, len(chunks))):
        begin(j)
    gain_flight = gain_copies(0)
    for copy in gain_flight:
        copy.start()
    for step in range(len(chunks) + LAG * (m - 1)):
        if step + RUN < len(chunks):
            begin(step + RUN)
        if step % 2 == 1 and step // 2 <= k:
            turn = step // 2
            for copy in gain_flight:
                copy.wait()
            total = (gains if turn == 0 else gain_held[turn - 1])[...]
            for i in range(len(gain_flight)):
                total = total + gain_landed[turn][i]
            if turn < k:
                gain_held[turn][...] = total
                gain_flight = gain_copies(turn + 1)
                for copy in gain_flight:
                    copy.start()
            else:
                gain_out[...] = total
        for stage in range(m - 1, -1, -1):
            j = step - LAG * stage
            if not 0 <= j < len(chunks):
                continue
            if stage == 0:
                own[j].wait()
            for copy in flights[j][stage]:
                copy.wait_recv()
            copy = add_up(j, stage)
            if stage < m - 1:
                following = copies_of(j, stage + 1)
                for copy in following:
                    copy.start()
                flights[j].append(following)
            else:
                crossing.append(copy)
    for copy in crossing:
        copy.wait_recv()
    for flight in flights:
        for copies in flight:
            for copy in copies:
                copy.wait_send()
    for copy in crossing:
        copy.wait_send()


def reduce_weights(grads, layouts, widths, gains, collective_id):
    sizes = split_dims(lax.axis_size("dp"))
    tensor_size = lax.axis_size("tensor")
    k = len(sizes)
    m = k - 1
    rows = grads[0].shape[0] // math.prod(sizes)
    chunks = pieces(layouts)
    peers = sum(size - 1 for size in sizes)
    n_in, n_out = len(grads), len(widths)
    held, landed, crossed = [], [], []
    for _, _, width, _, _, gather_order in chunks:
        order = tuple(reversed(gather_order))
        for stage in range(m):
            left = tuple(sizes[i] for i in range(k) if i not in order[: stage + 1])
            if stage < m - 1:
                held.append(pltpu.VMEM(left + (rows, width), jnp.bfloat16))
            landed.append(pltpu.VMEM((sizes[order[stage]] - 1,) + left + (rows, width), jnp.bfloat16))
        crossed.append(pltpu.VMEM((rows, width), jnp.float32))
    gain_landed = [pltpu.VMEM((size - 1,) + gains.shape, jnp.float32) for size in sizes + (tensor_size,)]
    whole = pl.BlockSpec(memory_space=pltpu.VMEM)
    outs = pl.pallas_call(
        functools.partial(reduce_kernel, sizes, chunks, (n_in, n_out), tensor_size),
        out_shape=[jax.ShapeDtypeStruct((rows, width), jnp.float32) for width in widths]
        + [jax.ShapeDtypeStruct(gains.shape, jnp.float32)],
        in_specs=[pl.BlockSpec(memory_space=pl.ANY)] * n_in + [whole],
        out_specs=[whole] * (n_out + 1),
        scratch_shapes=held
        + landed
        + crossed
        + [pltpu.VMEM(gains.shape, jnp.float32)] * k
        + gain_landed
        + [
            pltpu.SemaphoreType.DMA((len(chunks), peers)),
            pltpu.SemaphoreType.DMA((len(chunks), peers)),
            pltpu.SemaphoreType.DMA((len(chunks),)),
            pltpu.SemaphoreType.DMA((peers + tensor_size - 1,)),
            pltpu.SemaphoreType.DMA((peers + tensor_size - 1,)),
        ],
        compiler_params=pltpu.CompilerParams(
            collective_id=collective_id, has_side_effects=True, vmem_limit_bytes=VMEM_LIMIT
        ),
    )(*[g.reshape(sizes + (rows, g.shape[1])) for g in grads], gains)
    return outs[:n_out], outs[n_out]


def group_place():
    sizes = split_dims(lax.axis_size("dp"))
    place = Place(sizes)
    tensor_me = lax.axis_index("tensor")
    near = {"tensor": 1 - tensor_me}
    far = {"dp": place.peer(PAIR, 1)}
    return place.coords[PAIR], place.other(PAIR, 1), tensor_me, near, far


def group_barrier(near, far):
    barrier = pltpu.get_barrier_semaphore()
    pl.semaphore_signal(barrier, inc=1, device_id=near, device_id_type=MESH)
    pl.semaphore_signal(barrier, inc=1, device_id=far, device_id_type=MESH)
    pl.semaphore_wait(barrier, 2)


def gather_rows_kernel(in_ref, out_ref, send_sem, recv_sem):
    mine, theirs, tensor_me, near, far = group_place()
    group_barrier(near, far)
    rows = in_ref.shape[0] // 2
    across, beside, passed = [], [], []
    for i in range(2):
        source = in_ref.at[pl.ds(i * rows, rows)]
        slot = out_ref.at[mine, tensor_me, pl.ds(i * rows, rows)]
        across.append(remote(source, slot, send_sem.at[0, i], recv_sem.at[0, i], far))
        beside.append(remote(source, slot, send_sem.at[1, i], recv_sem.at[1, i], near))
        across[-1].start()
        beside[-1].start()
    out_ref[mine, tensor_me] = in_ref[...]
    for i in range(2):
        across[i].wait()
        slot = out_ref.at[theirs, tensor_me, pl.ds(i * rows, rows)]
        passed.append(remote(slot, slot, send_sem.at[2, i], recv_sem.at[2, i], near))
        passed[-1].start()
    for copy in beside + passed:
        copy.wait()


def gather_rows(values, collective_id):
    out = pl.pallas_call(
        gather_rows_kernel,
        out_shape=jax.ShapeDtypeStruct((2, 2) + values.shape, values.dtype),
        in_specs=[pl.BlockSpec(memory_space=pltpu.VMEM)],
        out_specs=pl.BlockSpec(memory_space=pltpu.VMEM),
        scratch_shapes=[pltpu.SemaphoreType.DMA((3, 2))] * 2,
        compiler_params=pltpu.CompilerParams(collective_id=collective_id, has_side_effects=True),
    )(values)
    return out.reshape(-1, values.shape[-1])


def scatter_rows_kernel(count, *refs):
    refs = list(refs)
    ins = [refs.pop(0) for _ in range(count)]
    outs = [refs.pop(0) for _ in range(count)]
    landed = [refs.pop(0) for _ in range(count)]
    sent = [refs.pop(0) for _ in range(count)]
    got = [refs.pop(0) for _ in range(count)]
    send_sem, recv_sem = refs
    mine, theirs, tensor_me, near, far = group_place()
    group_barrier(near, far)
    parts = 2
    rows = outs[0].shape[0] // parts
    first, second, across = [], [], []

    def span(part):
        return pl.ds(part * rows, rows)

    for i in range(count):
        for part in range(parts):
            copy = remote(
                ins[i].at[theirs, 1 - tensor_me, span(part)],
                landed[i].at[0, span(part)],
                send_sem.at[i, 0, part],
                recv_sem.at[i, 0, part],
                near,
            )
            copy.start()
            first.append(copy)
        copy = remote(
            ins[i].at[mine, 1 - tensor_me],
            landed[i].at[1],
            send_sem.at[i, 1, 0],
            recv_sem.at[i, 1, 0],
            near,
        )
        copy.start()
        second.append(copy)
    for i in range(count):
        for part in range(parts):
            first[i * parts + part].wait_recv()

            def body(r, carry):
                at = pl.ds(pl.multiple_of(part * rows + r * 16, 16), 16)
                total = ins[i][theirs, tensor_me, at, :] + landed[i][0, at, :]
                sent[i][at, :] = total.astype(jnp.bfloat16)
                return carry

            lax.fori_loop(0, rows // 16, body, 0)
            copy = remote(
                sent[i].at[span(part)],
                got[i].at[span(part)],
                send_sem.at[i, 2, part],
                recv_sem.at[i, 2, part],
                far,
            )
            copy.start()
            across.append(copy)
    for i in range(count):
        second[i].wait_recv()
        for part in range(parts):
            across[i * parts + part].wait_recv()

            def body(r, carry):
                at = pl.ds(pl.multiple_of(part * rows + r * 16, 16), 16)
                total = ins[i][mine, tensor_me, at, :] + landed[i][1, at, :]
                outs[i][at, :] = total + got[i][at, :].astype(jnp.float32)
                return carry

            lax.fori_loop(0, rows // 16, body, 0)
    for copy in first + second + across:
        copy.wait_send()


def scatter_rows(partials, collective_id):
    count = len(partials)
    rows, width = partials[0].shape[0] // 4, partials[0].shape[1]
    whole = pl.BlockSpec(memory_space=pltpu.VMEM)
    return pl.pallas_call(
        functools.partial(scatter_rows_kernel, count),
        out_shape=[jax.ShapeDtypeStruct((rows, width), jnp.float32)] * count,
        in_specs=[whole] * count,
        out_specs=[whole] * count,
        scratch_shapes=[pltpu.VMEM((2, rows, width), jnp.float32)] * count
        + [pltpu.VMEM((rows, width), jnp.bfloat16)] * (2 * count)
        + [pltpu.SemaphoreType.DMA((count, 3, 2))] * 2,
        compiler_params=pltpu.CompilerParams(
            collective_id=collective_id, has_side_effects=True, vmem_limit_bytes=VMEM_LIMIT
        ),
    )(*[p.reshape(2, 2, rows, width) for p in partials])


def turn(values, cosine, sine_part):
    return values * cosine + pltpu.roll(values, HEAD_SIZE // 2, 1) * sine_part


def dot_rows(left, right):
    return jnp.dot(left, right, preferred_element_type=jnp.float32)


def head_at(index):
    return slice(index * HEAD_SIZE, (index + 1) * HEAD_SIZE)


def attend_kernel(
    lengths, x, w, wo, gain_q, gain_k, cosine, sine_part,
    raw, rot, value, mixed, probs, out,
):
    length_rows = x.shape[0] // 2
    kv_heads = value.shape[1] // HEAD_SIZE
    ratio = mixed.shape[1] // value.shape[1]
    q_heads = kv_heads * ratio
    wide = 2 * HEAD_SIZE
    scaling = HEAD_SIZE ** (-0.5)
    row = lax.broadcasted_iota(jnp.int32, (length_rows, length_rows), 0)
    column = lax.broadcasted_iota(jnp.int32, (length_rows, length_rows), 1)
    for s in range(2):
        rows = slice(s * length_rows, (s + 1) * length_rows)
        x_rows = x[rows, :]
        for block in range(w.shape[1] // wide):
            at = slice(block * wide, (block + 1) * wide)
            projected = dot_rows(x_rows, w[:, at])
            if at.start < raw.shape[1]:
                raw[rows, at] = projected
            else:
                value[rows, at.start - raw.shape[1] : at.stop - raw.shape[1]] = projected.astype(
                    jnp.bfloat16
                )
        for head in range(q_heads + kv_heads):
            part = raw[rows, head_at(head)]
            gain = (gain_q if head < q_heads else gain_k)[...]
            normed, _ = rms_rows(part, gain)
            rot[rows, head_at(head)] = turn(normed, cosine[rows, :], sine_part[rows, :]).astype(
                jnp.bfloat16
            )
        live = (row < lengths[s]) & (column <= row)
        allowed = live | (row == column)
        for head in range(q_heads):
            group = head // ratio
            scores = product_t(rot[rows, head_at(head)], rot[rows, head_at(q_heads + group)])
            scores = jnp.where(allowed, scores * scaling, -1e30)
            row_max = jnp.max(scores, axis=-1, keepdims=True)
            total = jnp.sum(jnp.exp(scores - row_max), axis=-1, keepdims=True)
            shares = jnp.exp(scores - (row_max + jnp.log(total)))
            probs[s * q_heads + head] = shares
            mixed[rows, head_at(head)] = dot_rows(
                shares.astype(jnp.bfloat16), value[rows, head_at(group)]
            ).astype(jnp.bfloat16)
        for block in range(wo.shape[0] // wide):
            at = slice(block * wide, (block + 1) * wide)
            out[rows, at] = product_t(mixed[rows, :], wo[at, :])


def attend(lengths, normed, full_qkv, full_out, gain_query, gain_key, cosine, sine_part):
    rows = normed.shape[0]
    mixed_width = full_out.shape[1]
    value_width = (full_qkv.shape[1] - mixed_width) // 2
    raw_width = mixed_width + value_width
    count = 2 * (mixed_width // HEAD_SIZE)
    whole = pl.BlockSpec(memory_space=pltpu.VMEM)
    return pl.pallas_call(
        attend_kernel,
        out_shape=[
            jax.ShapeDtypeStruct((rows, raw_width), jnp.float32),
            jax.ShapeDtypeStruct((rows, raw_width), jnp.bfloat16),
            jax.ShapeDtypeStruct((rows, value_width), jnp.bfloat16),
            jax.ShapeDtypeStruct((rows, mixed_width), jnp.bfloat16),
            jax.ShapeDtypeStruct((count, rows // 2, rows // 2), jnp.float32),
            jax.ShapeDtypeStruct((rows, full_out.shape[0]), jnp.float32),
        ],
        in_specs=[pl.BlockSpec(memory_space=pltpu.SMEM)] + [whole] * 7,
        out_specs=[whole] * 6,
        compiler_params=pltpu.CompilerParams(vmem_limit_bytes=VMEM_LIMIT // 2),
    )(
        lengths, normed, full_qkv, full_out, gain_query[None], gain_key[None], cosine, sine_part
    )


def attend_back_kernel(
    grad, w, wo, gain_q, gain_k, cosine, sine_part, raw, rot, value, mixed, probs,
    grad_qkv, terms, gain_q_out, gain_k_out, grad_mixed,
):
    length_rows = grad.shape[0] // 2
    kv_heads = value.shape[1] // HEAD_SIZE
    ratio = mixed.shape[1] // value.shape[1]
    q_heads = kv_heads * ratio
    wide = 2 * HEAD_SIZE
    scaling = HEAD_SIZE ** (-0.5)
    gain_q_out[...] = jnp.zeros_like(gain_q_out)
    gain_k_out[...] = jnp.zeros_like(gain_k_out)
    for s in range(2):
        rows = slice(s * length_rows, (s + 1) * length_rows)

        def finish(grad_rot, head):
            gain, gain_out = (gain_q, gain_q_out) if head < q_heads else (gain_k, gain_k_out)
            upstream = turn(grad_rot, cosine[rows, :], -sine_part[rows, :])
            part = raw[rows, head_at(head)]
            _, inverse = rms_rows(part, gain[...])
            grad_raw, grad_gain = rms_back(upstream, part, inverse, gain[...])
            grad_qkv[rows, head_at(head)] = grad_raw.astype(jnp.bfloat16)
            gain_out[...] += grad_gain[None]

        grad_rows = grad[rows, :]
        for block in range(wo.shape[1] // wide):
            at = slice(block * wide, (block + 1) * wide)
            grad_mixed[:, at] = dot_rows(grad_rows, wo[:, at]).astype(jnp.bfloat16)
        for group in range(kv_heads):
            grad_key, grad_value = None, None
            for member in range(ratio):
                head = group * ratio + member
                shares = probs[s * q_heads + head]
                upstream = grad_mixed[:, head_at(head)]
                share_grads = product_t(upstream, value[rows, head_at(group)])
                delta = jnp.sum(
                    upstream.astype(jnp.float32)
                    * mixed[rows, head_at(head)].astype(jnp.float32),
                    axis=-1,
                    keepdims=True,
                )
                grad_scores = (shares * (share_grads - delta) * scaling).astype(jnp.bfloat16)
                to_value = product_tn(shares.astype(jnp.bfloat16), upstream)
                to_key = product_tn(grad_scores, rot[rows, head_at(head)])
                grad_value = to_value if grad_value is None else grad_value + to_value
                grad_key = to_key if grad_key is None else grad_key + to_key
                finish(dot_rows(grad_scores, rot[rows, head_at(q_heads + group)]), head)
            finish(grad_key, q_heads + group)
            grad_qkv[rows, head_at(q_heads + kv_heads + group)] = grad_value.astype(jnp.bfloat16)
        for block in range(w.shape[0] // wide):
            at = slice(block * wide, (block + 1) * wide)
            terms[rows, at] = product_t(grad_qkv[rows, :], w[at, :])


def attend_back(grad_attn, full_qkv, full_out, gain_query, gain_key, cosine, sine_part, saved):
    rows = grad_attn.shape[0]
    whole = pl.BlockSpec(memory_space=pltpu.VMEM)
    grad_qkv, terms, gain_q, gain_k = pl.pallas_call(
        attend_back_kernel,
        out_shape=[
            jax.ShapeDtypeStruct((rows, full_qkv.shape[1]), jnp.bfloat16),
            jax.ShapeDtypeStruct((rows, full_qkv.shape[0]), jnp.float32),
            jax.ShapeDtypeStruct((1, HEAD_SIZE), jnp.float32),
            jax.ShapeDtypeStruct((1, HEAD_SIZE), jnp.float32),
        ],
        in_specs=[whole] * 12,
        out_specs=[whole] * 4,
        scratch_shapes=[pltpu.VMEM((rows // 2, full_out.shape[1]), jnp.bfloat16)],
        compiler_params=pltpu.CompilerParams(vmem_limit_bytes=VMEM_LIMIT // 2),
    )(
        grad_attn, full_qkv, full_out, gain_query[None], gain_key[None], cosine, sine_part, *saved
    )
    return grad_qkv, terms, gain_q[0], gain_k[0]


def per_device(
    tokens,
    cotangent,
    lengths,
    w_query,
    key_matrix,
    value_matrix,
    w_out,
    w_gate,
    w_up,
    w_down,
    gain_attn,
    gain_mlp,
    gain_query,
    gain_key,
):
    own_rows = tokens.shape[0]
    total_rows = own_rows * 2
    weights = (w_query, key_matrix, value_matrix, w_out, w_gate, w_up, w_down)
    halves = [w.shape[1] // 2 for w in weights]
    layouts = (
        ((0, halves[0]), (1, halves[1]), (2, halves[2])),
        ((3, halves[3]),),
        ((4, halves[4]), (5, halves[5])),
        ((6, halves[6]),),
    )
    own_index = lax.axis_index("tensor") * own_rows + jnp.arange(own_rows, dtype=jnp.int32)
    own_live = own_index < lengths[0]
    cot_live = jnp.where(own_live[:, None], cotangent, jnp.zeros_like(cotangent))
    token_values = tokens.astype(jnp.float32)
    attn_norm, attn_inverse = rms_rows(token_values, gain_attn)
    length_row = jnp.broadcast_to(lengths.astype(jnp.float32)[:, None], (8, HEAD_SIZE))
    fetched, row_sets, length_pair = gather_all(
        weights, layouts, (attn_norm.astype(jnp.bfloat16), cot_live), length_row, 0
    )
    full_qkv, full_out, full_gu, full_down = fetched
    normed, grad_result = row_sets
    length_pair = length_pair.astype(jnp.int32)
    indices = jnp.arange(total_rows, dtype=jnp.int32)
    positions = jnp.where(indices[None] < length_pair[:, None], indices[None], 0).reshape(-1)
    cosine, sine_part = rope_tables(positions, HEAD_SIZE)
    cosine = jnp.concatenate([cosine, cosine], axis=1)
    sine_part = jnp.concatenate([-sine_part, sine_part], axis=1)
    qk_raw, rotated, value_part, mixed_flat, probs, mixed_terms = attend(
        length_pair, normed, full_qkv, full_out, gain_query, gain_key, cosine, sine_part
    )
    resid = token_values + scatter_rows([mixed_terms], 7)[0]
    mlp_norm, mlp_inverse = rms_rows(resid, gain_mlp)
    mlp_in = gather_rows(mlp_norm.astype(jnp.bfloat16), 4)
    gate_up = jnp.dot(mlp_in, full_gu, preferred_element_type=jnp.float32)
    gate_proj, up_proj = gate_up[:, : halves[4]], gate_up[:, halves[4] :]
    activation = (jax.nn.silu(gate_proj) * up_proj).astype(jnp.bfloat16)
    grad_act = jnp.dot(grad_result, full_down, preferred_element_type=jnp.float32)
    sigma = jax.nn.sigmoid(gate_proj)
    grad_gate = (grad_act * up_proj * sigma * (1.0 + gate_proj * (1.0 - sigma))).astype(
        jnp.bfloat16
    )
    grad_up = (grad_act * gate_proj * sigma).astype(jnp.bfloat16)
    grad_gu = jnp.concatenate([grad_gate, grad_up], axis=1)
    grad_mlp_in, down_rows = scatter_rows(
        [product_t(grad_gu, full_gu), product_t(activation, full_down)], 8
    )
    result = (resid + down_rows).astype(jnp.bfloat16)
    grad_w_down = product_tn(grad_result, activation)
    grad_w_gu = product_tn(mlp_in, grad_gu)
    grad_resid_mlp, grad_gain_mlp = rms_back(grad_mlp_in, resid, mlp_inverse, gain_mlp)
    grad_resid = cot_live.astype(jnp.float32) + grad_resid_mlp
    grad_attn = gather_rows(grad_resid.astype(jnp.bfloat16), 6)
    grad_w_out = product_tn(grad_attn, mixed_flat)
    saved = (qk_raw, rotated, value_part, mixed_flat, probs)
    grad_qkv, normed_terms, grad_gain_query, grad_gain_key = attend_back(
        grad_attn, full_qkv, full_out, gain_query, gain_key, cosine, sine_part, saved
    )
    grad_w_qkv = product_tn(normed, grad_qkv)
    grad_normed = scatter_rows([normed_terms], 10)[0]
    grad_tokens_attn, grad_gain_attn = rms_back(grad_normed, token_values, attn_inverse, gain_attn)
    grad_tokens = grad_resid + grad_tokens_attn
    gain_parts = (grad_gain_attn, grad_gain_mlp, grad_gain_query, grad_gain_key)
    gain_rows = [part.reshape(-1, HEAD_SIZE) for part in gain_parts]
    used = sum(part.shape[0] for part in gain_rows)
    gain_rows.append(jnp.zeros((-used % 8, HEAD_SIZE), jnp.float32))
    weight_sums, gain_sum = reduce_weights(
        [g.astype(jnp.bfloat16) for g in (grad_w_qkv, grad_w_out, grad_w_gu, grad_w_down)],
        layouts,
        [w.shape[1] for w in weights],
        jnp.concatenate(gain_rows, axis=0),
        collective_id=1,
    )
    gain_totals, row = [], 0
    for part in gain_parts:
        taken = part.shape[0] // HEAD_SIZE
        gain_totals.append(gain_sum[row : row + taken].reshape(-1))
        row += taken
    return (result, grad_tokens, *weight_sums, *gain_totals)


def solution(mesh):
    in_specs = (
        P(("dp", "tensor"), None),
        P(("dp", "tensor"), None),
        P("dp"),
        P("dp", "tensor"),
        P("dp", "tensor"),
        P("dp", "tensor"),
        P("dp", "tensor"),
        P("dp", "tensor"),
        P("dp", "tensor"),
        P("dp", "tensor"),
        P(),
        P(),
        P(),
        P(),
    )
    out_specs = (
        P(("dp", "tensor"), None),
        P(("dp", "tensor"), None),
        P("dp", "tensor"),
        P("dp", "tensor"),
        P("dp", "tensor"),
        P("dp", "tensor"),
        P("dp", "tensor"),
        P("dp", "tensor"),
        P("dp", "tensor"),
        P(),
        P(),
        P(),
        P(),
    )
    return jax.shard_map(
        per_device, mesh=mesh, in_specs=in_specs, out_specs=out_specs, check_vma=False
    )
```

profile of v0, /device:TPU:0, one launch (start us, length us, event | category | flops | bytes accessed | tf_op | source)
XLA Modules:
  0.0 325.1 jit_solution(14254446914894724027)
XLA Ops:
  0.6 1.1 fusion
  1.7 1.8 fusion.2.refs_7_
  4.2 1.7 broadcast_select_fusion.refs_8_
  5.9 0.6 broadcast_in_dim.33.refs_9_
  6.5 85.5 %shard_map.237 = (bf16[2,2,2,2,64,1024]{5,4,3,2,1,0:T(8,128)(2,1)}, bf16[2,2,2,2,64,512]{5,4,3,2,1,0:T(8,128)(2,1)}, bf16[2,2,2,2,64,1536]{5,4,3,2,1,0:T(8,128)(...) custom-call(bf16[64,1024]{1,0:T(8,128)(2,1)} %refs_0_.1, ...), custom_call_target="tpu_custom_call" | custom-call | tf_op jit(solution)/shard_map/pallas_call | solution.py:266
  92.1 0.0 copy-start
  92.1 1.0 convert_reduce_fusion.lengths
  93.1 0.1 broadcast_bitcast_fusion
  93.2 1.0 fusion.9
  94.2 0.2 pad_maximum_fusion.1
  94.4 1.2 copy-done.3
  95.6 1.2 copy-done.11
  96.9 7.5 %shard_map.238 = (f32[512,768]{1,0:T(8,128)S(1)}, bf16[512,768]{1,0:T(8,128)(2,1)S(1)}, bf16[512,256]{1,0:T(8,128)(2,1)S(1)}, bf16[512,512]{1,0:T(8,128)(2,1)S(1...) custom-call(s32[2]{0:T(128)S(1)} %convert_reduce_fusion.lengths, bf16[512,1024]{1,0:T(8,128)(2,1)S(1)} %bitcast.68, ...), custom_call_target="tpu_custom_call" | custom-call | tf_op jit(solution)/shard_map/pallas_call | solution.py:764
  104.4 1.3 copy-done.5
  105.8 1.3 copy-done.8
  107.1 1.2 copy-done.9
  108.3 0.9 copy-done.13
  109.2 0.8 copy-done.15
  110.0 12.1 %shard_map.239 = f32[128,1024]{1,0:T(8,128)} custom-call(f32[2,2,128,1024]{3,2,1,0:T(8,128)} %bitcast.67), custom_call_target="tpu_custom_call" | custom-call | tf_op jit(solution)/shard_map/pallas_call | solution.py:682
  122.0 1.3 multiply_reduce_fusion.2
  123.3 0.8 copy-done.22
  124.1 0.8 multiply_convert_fusion.3.in_ref
  124.9 11.4 %shard_map.240 = bf16[2,2,128,1024]{3,2,1,0:T(8,128)(2,1)} custom-call(bf16[128,1024]{1,0:T(8,128)(2,1)} %multiply_convert_fusion.3.in_ref), custom_call_target="tpu_custom_call" | custom-call | tf_op jit(solution)/shard_map/pallas_call | solution.py:594
  136.3 4.1 %fusion.12 = f32[512,1536]{1,0:T(8,128)S(1)} fusion(bf16[512,1024]{1,0:T(8,128)(2,1)} %bitcast.79, bf16[1024,1536]{1,0:T(8,128)(2,1)} %bitcast.85), kind=kOutput, calls=%fused_computation.54 | convolution fusion | flops 1610612736 | bytes 7340032 | tf_op jit(solution)/shard_map/dot_general | solution.py:906
  140.5 0.0 copy-done.36
  140.5 0.0 copy-done.37
  140.5 1.5 multiply_convert_fusion.2
  142.0 0.1 pad_maximum_fusion
  142.1 0.7 copy-done.26
  142.9 0.2 copy-done.28
  143.1 1.6 copy-done.35
  144.7 3.2 fusion.13.refs_0_
  147.9 2.3 fusion.14.refs_1_
  150.2 19.2 %shard_map.241 = (f32[128,1024]{1,0:T(8,128)}, f32[128,1024]{1,0:T(8,128)}) custom-call(f32[2,2,128,1024]{3,2,1,0:T(8,128)} %fusion.13.refs_0_, f32[2,2,128,1024]{3,2,1,0:T(8,128)} %fusion.14.refs_1_), custom_call_target="tpu_custom_call" | custom-call | tf_op jit(solution)/shard_map/pallas_call | solution.py:682
  169.4 1.4 multiply_reduce_fusion
  170.8 2.7 fusion.11
  173.4 11.1 %shard_map.242 = bf16[2,2,128,1024]{3,2,1,0:T(8,128)(2,1)} custom-call(bf16[128,1024]{1,0:T(8,128)(2,1)} %get-tuple-element.71.in_ref), custom_call_target="tpu_custom_call" | custom-call | tf_op jit(solution)/shard_map/pallas_call | solution.py:594
  184.5 1.2 copy-done.1
  185.7 1.2 copy-done.4
  187.0 1.6 copy-done.6
  188.6 1.4 copy-done.10
  190.0 1.1 copy-done.14
  191.1 1.0 copy-done.16
  192.1 6.2 %shard_map.243 = (bf16[512,1024]{1,0:T(8,128)(2,1)S(1)}, f32[512,1024]{1,0:T(8,128)S(1)}, f32[1,128]{1,0:T(1,128)S(1)}, f32[1,128]{1,0:T(1,128)S(1)}) custom-call(bf16[512,1024]{1,0:T(8,128)(2,1)S(1)} %bitcast.62, bf16[1024,1024]{1,0:T(8,128)(2,1)S(1)} %bitcast.61, bf16[1024,512]{1,0:T(8,128)(2,1)S(1)} %bitcast.65, f32[1,128]{1,0:T(1,128)S(1)} %bitcast.71, ...), custom_call_target="tpu_custom_call" | custom-call | tf_op jit(solution)/shard_map/pallas_call | solution.py:839
  198.4 1.3 copy-done.7
  199.7 1.0 copy-done.20
  200.7 12.9 %shard_map.244 = f32[128,1024]{1,0:T(8,128)} custom-call(f32[2,2,128,1024]{3,2,1,0:T(8,128)} %bitcast.66), custom_call_target="tpu_custom_call" | custom-call | tf_op jit(solution)/shard_map/pallas_call | solution.py:682
  213.6 1.4 fusion.8
  215.0 2.1 fusion.5
  217.1 2.6 convolution_convert_fusion.1
  219.8 1.8 convolution_convert_fusion.3
  221.5 3.5 %convolution_convert_fusion = bf16[1024,1536]{1,0:T(8,128)(2,1)} fusion(bf16[512,1024]{1,0:T(8,128)(2,1)S(1)} %bitcast.80, bf16[512,768]{1,0:T(8,128)(2,1)S(1)} %copy-done.29, bf16[512,768]{1,0:T(8,128)(2,1)S(1)} %copy-done.27), kind=kOutput, calls=%fused_computation | convolution fusion | flops 1615331328 | bytes 5767168 | tf_op jit(solution)/shard_map/dot_general | solution.py:50
  225.0 2.2 convolution_convert_fusion.2
  227.2 1.8 concatenate.15.refs_4_
  229.0 84.7 %shard_map.245 = (f32[64,1024]{1,0:T(8,128)}, f32[64,512]{1,0:T(8,128)}, f32[64,512]{1,0:T(8,128)}, f32[64,1024]{1,0:T(8,128)}, f32[64,1536]{1,0:T(8,128)}, /*in...) custom-call(bf16[2,2,2,2,64,1024]{5,4,3,2,1,0:T(8,128)(2,1)} %bitcast.75, ...), custom_call_target="tpu_custom_call" | custom-call | tf_op jit(solution)/shard_map/pallas_call | solution.py:530
  313.7 1.4 slice_bitcast_fusion
  315.1 1.3 slice_bitcast_fusion.2
  316.4 1.7 copy.39
  318.1 1.6 copy.40
  319.7 1.6 copy.41
  321.2 1.7 copy.42
  322.9 0.7 copy.43
  323.6 0.7 copy.44
  324.4 0.7 copy.45
  (71 shorter events, 0.2 us)
Async XLA Ops:
  6.5 87.9 %copy-start.18 = (f32[128]{0:T(128)S(1)}, f32[128]{0:T(128)}, u32[]{:S(2)}) copy-start(f32[128]{0:T(128)} %param.26) | copy-start | bytes 1540
  6.5 87.9 %copy-start.19 = (f32[128]{0:T(128)S(1)}, f32[128]{0:T(128)}, u32[]{:S(2)}) copy-start(f32[128]{0:T(128)} %param.27) | copy-start | bytes 1540
  92.1 2.3 copy-start
  94.4 1.2 copy-start.3
  95.6 1.2 copy-start.11
  104.4 1.3 copy-start.5
  105.8 1.3 copy-start.8
  107.1 1.2 copy-start.9
  108.3 0.9 copy-start.13
  109.2 0.8 copy-start.15
  110.0 14.1 %copy-start.33 = (f32[1024]{0:T(1024)S(1)}, f32[1024]{0:T(1024)}, u32[]{:S(2)}) copy-start(f32[1024]{0:T(1024)} %param.25) | copy-start | bytes 12292
  123.3 0.8 copy-start.22
  136.3 4.2 %copy-start.36 = (bf16[2,2,2,2,64,768]{5,4,3,2,1,0:T(8,128)(2,1)S(1)}, bf16[2,2,2,2,64,768]{5,4,3,2,1,0:T(8,128)(2,1)}, u32[]{:S(2)}) copy-start(bf16[2,2,2,2,64,768]{5,4,3,2,1,0:T(8,128)(2,1)} %get-tuple-element.46) | copy-start | bytes 4718596
  136.3 4.2 %copy-start.37 = (bf16[2,2,128,1024]{3,2,1,0:T(8,128)(2,1)S(1)}, bf16[2,2,128,1024]{3,2,1,0:T(8,128)(2,1)}, u32[]{:S(2)}) copy-start(bf16[2,2,128,1024]{3,2,1,0:T(8,128)(2,1)} %get-tuple-element.45) | copy-start | bytes 3145732
  141.9 0.9 copy-start.26
  142.0 1.1 copy-start.28
  142.0 5.9 %copy-start.39 = (bf16[512,768]{1,0:T(8,128)(2,1)}, bf16[512,768]{1,0:T(8,128)(2,1)S(1)}, u32[]{:S(2)}) copy-start(bf16[512,768]{1,0:T(8,128)(2,1)S(1)} %get-tuple-element.77) | copy-start | bytes 2359300
  142.0 2.7 copy-start.35
  184.5 1.2 copy-start.1
  185.7 1.2 copy-start.4
  187.0 1.6 copy-start.6
  188.6 1.4 copy-start.10
  190.0 1.1 copy-start.14
  191.1 1.0 copy-start.16
  198.4 1.3 copy-start.7
  199.7 1.0 copy-start.20
  200.7 12.9 %copy-start.23 = (bf16[128,1024]{1,0:T(8,128)(2,1)S(1)}, bf16[128,1024]{1,0:T(8,128)(2,1)}, u32[]{:S(2)}) copy-start(bf16[128,1024]{1,0:T(8,128)(2,1)} %param.14) | copy-start | bytes 786436
  200.7 12.9 %copy-start.34 = (f32[1024]{0:T(1024)S(1)}, f32[1024]{0:T(1024)}, u32[]{:S(2)}) copy-start(f32[1024]{0:T(1024)} %param.24) | copy-start | bytes 12292
  200.7 14.3 %copy-start.24 = (f32[128,1024]{1,0:T(8,128)S(1)}, f32[128,1024]{1,0:T(8,128)}, u32[]{:S(2)}) copy-start(f32[128,1024]{1,0:T(8,128)} %get-tuple-element.72) | copy-start | bytes 1572868
  213.6 3.5 %copy-start.12 = (bf16[2,2,128,1024]{3,2,1,0:T(8,128)(2,1)S(1)}, bf16[2,2,128,1024]{3,2,1,0:T(8,128)(2,1)}, u32[]{:S(2)}) copy-start(bf16[2,2,128,1024]{3,2,1,0:T(8,128)(2,1)} %get-tuple-element.41) | copy-start | bytes 3145732
  213.6 3.5 %copy-start.21 = (bf16[512,1024]{1,0:T(8,128)(2,1)S(1)}, bf16[512,1024]{1,0:T(8,128)(2,1)}, u32[]{:S(2)}) copy-start(bf16[512,1024]{1,0:T(8,128)(2,1)} %copy-done.20) | copy-start | bytes 3145732
  217.1 2.7 copy-start.2
  217.1 2.7 copy-start.17
  219.8 1.8 copy-start.25
  219.8 1.8 copy-start.27
  219.8 1.8 copy-start.29
  221.5 3.5 %copy-start.38 = (bf16[2,2,128,1024]{3,2,1,0:T(8,128)(2,1)S(1)}, bf16[2,2,128,1024]{3,2,1,0:T(8,128)(2,1)}, u32[]{:S(2)}) copy-start(bf16[2,2,128,1024]{3,2,1,0:T(8,128)(2,1)} %get-tuple-element.45) | copy-start | bytes 3145732
  221.5 3.5 %copy-start.40 = (bf16[512,768]{1,0:T(8,128)(2,1)S(1)}, bf16[512,768]{1,0:T(8,128)(2,1)}, u32[]{:S(2)}) copy-start(bf16[512,768]{1,0:T(8,128)(2,1)} %copy-done.39) | copy-start | bytes 2359300
  313.7 9.2 %copy-start.32 = (f32[64,1536]{1,0:T(8,128)S(1)}, f32[64,1536]{1,0:T(8,128)}, u32[]{:S(2)}) copy-start(f32[64,1536]{1,0:T(8,128)} %get-tuple-element.111) | copy-start | bytes 1179652
  313.7 9.9 %copy-start.31 = (f32[64,1536]{1,0:T(8,128)S(1)}, f32[64,1536]{1,0:T(8,128)}, u32[]{:S(2)}) copy-start(f32[64,1536]{1,0:T(8,128)} %get-tuple-element.112) | copy-start | bytes 1179652
  316.4 8.0 %copy-start.30 = (f32[64,1536]{1,0:T(8,128)S(1)}, f32[64,1536]{1,0:T(8,128)}, u32[]{:S(2)}) copy-start(f32[64,1536]{1,0:T(8,128)} %get-tuple-element.113) | copy-start | bytes 1179652
where the time goes:
time: 326 us; the launch traced here: 325 us
  Pallas kernels  251 us (77%)
  local copies, waits for them, and re-layouts  35.2 us (11%)
  matrix products  21.2 us (7%)
  other arithmetic  16.5 us (5%)
    pallas_call x1, Pallas kernels, gather_all(): pl.pallas_call(functools.partial(gather_kernel, sizes, chunks, (n_in, n_o...  85.5 us
    pallas_call x1, Pallas kernels, reduce_weights(): pl.pallas_call(functools.partial(reduce_kernel, sizes, chunks, (n_in, n_o...  84.7 us
    pallas_call x3, Pallas kernels, scatter_rows(): pl.pallas_call(functools.partial(scatter_rows_kernel, count), out_shape=[...  44.1 us
    unnamed x93, local copies, waits for them, and re-layouts  30.2 us
    pallas_call x2, Pallas kernels, gather_rows(): pl.pallas_call(gather_rows_kernel, out_shape=jax.ShapeDtypeStruct((2, 2)...  22.5 us
    dot_general x4, matrix products, product_tn(): lax.dot_general(left, right, (((0,), (0,)), ((), ())), preferred_element_...  10.1 us
    pallas_call x1, Pallas kernels, attend(): pl.pallas_call(attend_kernel, out_shape=[jax.ShapeDtypeStruct((rows, raw_...  7.53 us

commit v1 on v0

--- a/solution.py
+++ b/solution.py
@@ -57,6 +57,7 @@
 
 
 PAIR = 1
+PARTS = 4
 AHEAD = 5
 DEPTH = 2
 RUN = 3
@@ -571,9 +572,9 @@
 def gather_rows_kernel(in_ref, out_ref, send_sem, recv_sem):
     mine, theirs, tensor_me, near, far = group_place()
     group_barrier(near, far)
-    rows = in_ref.shape[0] // 2
+    rows = in_ref.shape[0] // PARTS
     across, beside, passed = [], [], []
-    for i in range(2):
+    for i in range(PARTS):
         source = in_ref.at[pl.ds(i * rows, rows)]
         slot = out_ref.at[mine, tensor_me, pl.ds(i * rows, rows)]
         across.append(remote(source, slot, send_sem.at[0, i], recv_sem.at[0, i], far))
@@ -581,7 +582,7 @@
         across[-1].start()
         beside[-1].start()
     out_ref[mine, tensor_me] = in_ref[...]
-    for i in range(2):
+    for i in range(PARTS):
         across[i].wait()
         slot = out_ref.at[theirs, tensor_me, pl.ds(i * rows, rows)]
         passed.append(remote(slot, slot, send_sem.at[2, i], recv_sem.at[2, i], near))
@@ -596,7 +597,7 @@
         out_shape=jax.ShapeDtypeStruct((2, 2) + values.shape, values.dtype),
         in_specs=[pl.BlockSpec(memory_space=pltpu.VMEM)],
         out_specs=pl.BlockSpec(memory_space=pltpu.VMEM),
-        scratch_shapes=[pltpu.SemaphoreType.DMA((3, 2))] * 2,
+        scratch_shapes=[pltpu.SemaphoreType.DMA((3, PARTS))] * 2,
         compiler_params=pltpu.CompilerParams(collective_id=collective_id, has_side_effects=True),
     )(values)
     return out.reshape(-1, values.shape[-1])
@@ -612,7 +613,7 @@
     send_sem, recv_sem = refs
     mine, theirs, tensor_me, near, far = group_place()
     group_barrier(near, far)
-    parts = 2
+    parts = PARTS
     rows = outs[0].shape[0] // parts
     first, second, across = [], [], []
 
@@ -686,7 +687,7 @@
         out_specs=[whole] * count,
         scratch_shapes=[pltpu.VMEM((2, rows, width), jnp.float32)] * count
         + [pltpu.VMEM((rows, width), jnp.bfloat16)] * (2 * count)
-        + [pltpu.SemaphoreType.DMA((count, 3, 2))] * 2,
+        + [pltpu.SemaphoreType.DMA((count, 3, PARTS))] * 2,
         compiler_params=pltpu.CompilerParams(
             collective_id=collective_id, has_side_effects=True, vmem_limit_bytes=VMEM_LIMIT
         ),

time: 326 us -> 327 us (level)
  no operation moved by 1% of the time
where the time goes in v1:
time: 327 us; the launch traced here: 326 us
  Pallas kernels  251 us (77%)
  local copies, waits for them, and re-layouts  35.2 us (11%)
  matrix products  21.2 us (6%)
  other arithmetic  16.5 us (5%)
    pallas_call x1, Pallas kernels, gather_all(): pl.pallas_call(functools.partial(gather_kernel, sizes, chunks, (n_in, n_o...  85.5 us
    pallas_call x1, Pallas kernels, reduce_weights(): pl.pallas_call(functools.partial(reduce_kernel, sizes, chunks, (n_in, n_o...  85.4 us
    pallas_call x3, Pallas kernels, scatter_rows(): pl.pallas_call(functools.partial(scatter_rows_kernel, count), out_shape=[...  43.9 us
    unnamed x93, local copies, waits for them, and re-layouts  30.2 us
    pallas_call x2, Pallas kernels, gather_rows(): pl.pallas_call(gather_rows_kernel, out_shape=jax.ShapeDtypeStruct((2, 2)...  22.5 us
    dot_general x4, matrix products, product_tn(): lax.dot_general(left, right, (((0,), (0,)), ((), ())), preferred_element_...  10.1 us
    pallas_call x1, Pallas kernels, attend(): pl.pallas_call(attend_kernel, out_shape=[jax.ShapeDtypeStruct((rows, raw_...  7.53 us

profile of v1, /device:TPU:0, one launch (start us, length us, event | category | flops | bytes accessed | tf_op | source)
XLA Modules:
  0.0 325.7 jit_solution(17420654533004022877)
XLA Ops:
  0.6 1.1 fusion
  1.7 1.8 fusion.2.refs_7_
  4.2 1.7 broadcast_select_fusion.refs_8_
  5.9 0.6 broadcast_in_dim.33.refs_9_
  6.5 85.5 %shard_map.237 = (bf16[2,2,2,2,64,1024]{5,4,3,2,1,0:T(8,128)(2,1)}, bf16[2,2,2,2,64,512]{5,4,3,2,1,0:T(8,128)(2,1)}, bf16[2,2,2,2,64,1536]{5,4,3,2,1,0:T(8,128)(...) custom-call(bf16[64,1024]{1,0:T(8,128)(2,1)} %refs_0_.1, ...), custom_call_target="tpu_custom_call" | custom-call | tf_op jit(solution)/shard_map/pallas_call | solution.py:267
  92.1 0.0 copy-start
  92.1 1.0 convert_reduce_fusion.lengths
  93.1 0.1 broadcast_bitcast_fusion
  93.2 1.0 fusion.9
  94.2 0.2 pad_maximum_fusion.1
  94.4 1.2 copy-done.3
  95.6 1.2 copy-done.11
  96.9 7.5 %shard_map.238 = (f32[512,768]{1,0:T(8,128)S(1)}, bf16[512,768]{1,0:T(8,128)(2,1)S(1)}, bf16[512,256]{1,0:T(8,128)(2,1)S(1)}, bf16[512,512]{1,0:T(8,128)(2,1)S(1...) custom-call(s32[2]{0:T(128)S(1)} %convert_reduce_fusion.lengths, bf16[512,1024]{1,0:T(8,128)(2,1)S(1)} %bitcast.68, ...), custom_call_target="tpu_custom_call" | custom-call | tf_op jit(solution)/shard_map/pallas_call | solution.py:765
  104.4 1.3 copy-done.5
  105.8 1.3 copy-done.8
  107.1 1.2 copy-done.9
  108.3 0.9 copy-done.13
  109.2 0.8 copy-done.15
  110.0 11.9 %shard_map.239 = f32[128,1024]{1,0:T(8,128)} custom-call(f32[2,2,128,1024]{3,2,1,0:T(8,128)} %bitcast.67), custom_call_target="tpu_custom_call" | custom-call | tf_op jit(solution)/shard_map/pallas_call | solution.py:683
  121.9 1.3 multiply_reduce_fusion.2
  123.2 0.8 copy-done.22
  124.0 0.8 multiply_convert_fusion.3.in_ref
  124.8 11.4 %shard_map.240 = bf16[2,2,128,1024]{3,2,1,0:T(8,128)(2,1)} custom-call(bf16[128,1024]{1,0:T(8,128)(2,1)} %multiply_convert_fusion.3.in_ref), custom_call_target="tpu_custom_call" | custom-call | tf_op jit(solution)/shard_map/pallas_call | solution.py:595
  136.2 4.1 %fusion.12 = f32[512,1536]{1,0:T(8,128)S(1)} fusion(bf16[512,1024]{1,0:T(8,128)(2,1)} %bitcast.79, bf16[1024,1536]{1,0:T(8,128)(2,1)} %bitcast.85), kind=kOutput, calls=%fused_computation.54 | convolution fusion | flops 1610612736 | bytes 7340032 | tf_op jit(solution)/shard_map/dot_general | solution.py:907
  140.4 1.5 multiply_convert_fusion.2
  141.9 0.0 copy-start.26
  141.9 0.0 copy-start.28
  141.9 0.1 pad_maximum_fusion
  142.0 0.7 copy-done.26
  142.8 0.2 copy-done.28
  143.0 1.6 copy-done.35
  144.6 3.2 fusion.13.refs_0_
  147.8 2.3 fusion.14.refs_1_
  150.1 19.2 %shard_map.241 = (f32[128,1024]{1,0:T(8,128)}, f32[128,1024]{1,0:T(8,128)}) custom-call(f32[2,2,128,1024]{3,2,1,0:T(8,128)} %fusion.13.refs_0_, f32[2,2,128,1024]{3,2,1,0:T(8,128)} %fusion.14.refs_1_), custom_call_target="tpu_custom_call" | custom-call | tf_op jit(solution)/shard_map/pallas_call | solution.py:683
  169.3 1.4 multiply_reduce_fusion
  170.7 2.7 fusion.11
  173.3 11.1 %shard_map.242 = bf16[2,2,128,1024]{3,2,1,0:T(8,128)(2,1)} custom-call(bf16[128,1024]{1,0:T(8,128)(2,1)} %get-tuple-element.71.in_ref), custom_call_target="tpu_custom_call" | custom-call | tf_op jit(solution)/shard_map/pallas_call | solution.py:595
  184.5 1.2 copy-done.1
  185.7 1.2 copy-done.4
  186.9 1.6 copy-done.6
  188.5 1.4 copy-done.10
  189.9 1.1 copy-done.14
  191.0 1.0 copy-done.16
  192.1 6.2 %shard_map.243 = (bf16[512,1024]{1,0:T(8,128)(2,1)S(1)}, f32[512,1024]{1,0:T(8,128)S(1)}, f32[1,128]{1,0:T(1,128)S(1)}, f32[1,128]{1,0:T(1,128)S(1)}) custom-call(bf16[512,1024]{1,0:T(8,128)(2,1)S(1)} %bitcast.62, bf16[1024,1024]{1,0:T(8,128)(2,1)S(1)} %bitcast.61, bf16[1024,512]{1,0:T(8,128)(2,1)S(1)} %bitcast.65, f32[1,128]{1,0:T(1,128)S(1)} %bitcast.71, ...), custom_call_target="tpu_custom_call" | custom-call | tf_op jit(solution)/shard_map/pallas_call | solution.py:840
  198.3 1.3 copy-done.7
  199.6 1.0 copy-done.20
  200.6 12.8 %shard_map.244 = f32[128,1024]{1,0:T(8,128)} custom-call(f32[2,2,128,1024]{3,2,1,0:T(8,128)} %bitcast.66), custom_call_target="tpu_custom_call" | custom-call | tf_op jit(solution)/shard_map/pallas_call | solution.py:683
  213.4 1.4 fusion.8
  214.8 2.1 fusion.5
  216.9 2.6 convolution_convert_fusion.1
  219.6 1.8 convolution_convert_fusion.3
  221.4 3.5 %convolution_convert_fusion = bf16[1024,1536]{1,0:T(8,128)(2,1)} fusion(bf16[512,1024]{1,0:T(8,128)(2,1)S(1)} %bitcast.80, bf16[512,768]{1,0:T(8,128)(2,1)S(1)} %copy-done.29, bf16[512,768]{1,0:T(8,128)(2,1)S(1)} %copy-done.27), kind=kOutput, calls=%fused_computation | convolution fusion | flops 1615331328 | bytes 5767168 | tf_op jit(solution)/shard_map/dot_general | solution.py:50
  224.8 2.2 convolution_convert_fusion.2
  227.1 1.8 concatenate.15.refs_4_
  228.8 85.4 %shard_map.245 = (f32[64,1024]{1,0:T(8,128)}, f32[64,512]{1,0:T(8,128)}, f32[64,512]{1,0:T(8,128)}, f32[64,1024]{1,0:T(8,128)}, f32[64,1536]{1,0:T(8,128)}, /*in...) custom-call(bf16[2,2,2,2,64,1024]{5,4,3,2,1,0:T(8,128)(2,1)} %bitcast.75, ...), custom_call_target="tpu_custom_call" | custom-call | tf_op jit(solution)/shard_map/pallas_call | solution.py:531
  314.3 1.4 slice_bitcast_fusion
  315.7 1.3 slice_bitcast_fusion.2
  316.9 1.7 copy.39
  318.7 1.6 copy.40
  320.2 1.6 copy.41
  321.8 1.7 copy.42
  323.5 0.7 copy.43
  324.2 0.7 copy.44
  325.0 0.7 copy.45
  (71 shorter events, 0.2 us)
Async XLA Ops:
  6.5 87.9 %copy-start.18 = (f32[128]{0:T(128)S(1)}, f32[128]{0:T(128)}, u32[]{:S(2)}) copy-start(f32[128]{0:T(128)} %param.26) | copy-start | bytes 1540
  6.5 87.9 %copy-start.19 = (f32[128]{0:T(128)S(1)}, f32[128]{0:T(128)}, u32[]{:S(2)}) copy-start(f32[128]{0:T(128)} %param.27) | copy-start | bytes 1540
  92.1 2.3 copy-start
  94.4 1.2 copy-start.3
  95.6 1.2 copy-start.11
  104.4 1.3 copy-start.5
  105.8 1.3 copy-start.8
  107.1 1.2 copy-start.9
  108.3 0.9 copy-start.13
  109.2 0.8 copy-start.15
  110.0 14.0 %copy-start.33 = (f32[1024]{0:T(1024)S(1)}, f32[1024]{0:T(1024)}, u32[]{:S(2)}) copy-start(f32[1024]{0:T(1024)} %param.25) | copy-start | bytes 12292
  123.2 0.8 copy-start.22
  136.2 4.2 %copy-start.36 = (bf16[2,2,2,2,64,768]{5,4,3,2,1,0:T(8,128)(2,1)S(1)}, bf16[2,2,2,2,64,768]{5,4,3,2,1,0:T(8,128)(2,1)}, u32[]{:S(2)}) copy-start(bf16[2,2,2,2,64,768]{5,4,3,2,1,0:T(8,128)(2,1)} %get-tuple-element.46) | copy-start | bytes 4718596
  136.2 4.2 %copy-start.37 = (bf16[2,2,128,1024]{3,2,1,0:T(8,128)(2,1)S(1)}, bf16[2,2,128,1024]{3,2,1,0:T(8,128)(2,1)}, u32[]{:S(2)}) copy-start(bf16[2,2,128,1024]{3,2,1,0:T(8,128)(2,1)} %get-tuple-element.45) | copy-start | bytes 3145732
  141.9 0.9 copy-start.26
  141.9 1.1 copy-start.28
  141.9 5.9 %copy-start.39 = (bf16[512,768]{1,0:T(8,128)(2,1)}, bf16[512,768]{1,0:T(8,128)(2,1)S(1)}, u32[]{:S(2)}) copy-start(bf16[512,768]{1,0:T(8,128)(2,1)S(1)} %get-tuple-element.77) | copy-start | bytes 2359300
  141.9 2.7 copy-start.35
  184.4 1.2 copy-start.1
  185.7 1.2 copy-start.4
  186.9 1.6 copy-start.6
  188.5 1.4 copy-start.10
  189.9 1.1 copy-start.14
  191.0 1.0 copy-start.16
  198.3 1.3 copy-start.7
  199.6 1.0 copy-start.20
  200.6 12.8 %copy-start.23 = (bf16[128,1024]{1,0:T(8,128)(2,1)S(1)}, bf16[128,1024]{1,0:T(8,128)(2,1)}, u32[]{:S(2)}) copy-start(bf16[128,1024]{1,0:T(8,128)(2,1)} %param.14) | copy-start | bytes 786436
  200.6 12.8 %copy-start.34 = (f32[1024]{0:T(1024)S(1)}, f32[1024]{0:T(1024)}, u32[]{:S(2)}) copy-start(f32[1024]{0:T(1024)} %param.24) | copy-start | bytes 12292
  200.6 14.2 %copy-start.24 = (f32[128,1024]{1,0:T(8,128)S(1)}, f32[128,1024]{1,0:T(8,128)}, u32[]{:S(2)}) copy-start(f32[128,1024]{1,0:T(8,128)} %get-tuple-element.72) | copy-start | bytes 1572868
  213.4 3.5 %copy-start.12 = (bf16[2,2,128,1024]{3,2,1,0:T(8,128)(2,1)S(1)}, bf16[2,2,128,1024]{3,2,1,0:T(8,128)(2,1)}, u32[]{:S(2)}) copy-start(bf16[2,2,128,1024]{3,2,1,0:T(8,128)(2,1)} %get-tuple-element.41) | copy-start | bytes 3145732
  213.4 3.5 %copy-start.21 = (bf16[512,1024]{1,0:T(8,128)(2,1)S(1)}, bf16[512,1024]{1,0:T(8,128)(2,1)}, u32[]{:S(2)}) copy-start(bf16[512,1024]{1,0:T(8,128)(2,1)} %copy-done.20) | copy-start | bytes 3145732
  216.9 2.7 copy-start.2
  216.9 2.7 copy-start.17
  219.6 1.8 copy-start.25
  219.6 1.8 copy-start.27
  219.6 1.8 copy-start.29
  221.3 3.5 %copy-start.38 = (bf16[2,2,128,1024]{3,2,1,0:T(8,128)(2,1)S(1)}, bf16[2,2,128,1024]{3,2,1,0:T(8,128)(2,1)}, u32[]{:S(2)}) copy-start(bf16[2,2,128,1024]{3,2,1,0:T(8,128)(2,1)} %get-tuple-element.45) | copy-start | bytes 3145732
  221.3 3.5 %copy-start.40 = (bf16[512,768]{1,0:T(8,128)(2,1)S(1)}, bf16[512,768]{1,0:T(8,128)(2,1)}, u32[]{:S(2)}) copy-start(bf16[512,768]{1,0:T(8,128)(2,1)} %copy-done.39) | copy-start | bytes 2359300
  314.3 9.2 %copy-start.32 = (f32[64,1536]{1,0:T(8,128)S(1)}, f32[64,1536]{1,0:T(8,128)}, u32[]{:S(2)}) copy-start(f32[64,1536]{1,0:T(8,128)} %get-tuple-element.111) | copy-start | bytes 1179652
  314.3 9.9 %copy-start.31 = (f32[64,1536]{1,0:T(8,128)S(1)}, f32[64,1536]{1,0:T(8,128)}, u32[]{:S(2)}) copy-start(f32[64,1536]{1,0:T(8,128)} %get-tuple-element.112) | copy-start | bytes 1179652
  316.9 8.0 %copy-start.30 = (f32[64,1536]{1,0:T(8,128)S(1)}, f32[64,1536]{1,0:T(8,128)}, u32[]{:S(2)}) copy-start(f32[64,1536]{1,0:T(8,128)} %get-tuple-element.113) | copy-start | bytes 1179652
